TPU v7x, 32 devices: a whole 2x2x4 slice. The times are simulated.
32 devices in a mesh: section: 4 (over y, x), tile: 8 (over z, core).
Axes of the slice: x: 2, y: 2, z: 4, core: 2. Of those that a mesh axis runs over, the one named last changes fastest.
Arguments:
- stored_inputs: bfloat16 [4, 4, 24, 128, 1024], P('section', None, 'tile'), may hold values from -6 to 6
- cotangent: bfloat16 [4, 24, 128, 1024], P(None, 'tile'), may hold values from -6 to 6
- w_reduce: bfloat16 [4, 1024, 256], P('section'), may hold values from -0.1875 to 0.1875
- w_spatial: bfloat16 [4, 2304, 256], P('section'), may hold values from -0.125 to 0.125
- w_expand: bfloat16 [4, 256, 1024], P('section'), may hold values from -0.375 to 0.375
- bias_reduce: float32 [4, 256], P('section'), may hold values from -1 to 1
- bias_spatial: float32 [4, 256], P('section'), may hold values from -1 to 1
- bias_expand: float32 [4, 1024], P('section'), may hold values from 0.5 to 2
Outputs:
- input_grads: bfloat16 [4, 4, 24, 128, 1024], P('section', None, 'tile')
- grad_reduce: float32 [4, 1024, 256], P('section', 'tile')
- grad_spatial: float32 [4, 2304, 256], P('section', 'tile')
- grad_expand: float32 [4, 256, 1024], P('section', 'tile')
All inputs are finite; a program needn't handle non-finite values.
Results may differ from a plain program's by a relative error of at most 0.024.
Values may be sent and summed in bfloat16 or wider, within the bound.
A program may use at most 64 MiB of HBM per device.

v0:
```python
import jax
import jax.numpy as jnp
from jax import lax
from jax.sharding import PartitionSpec as P


def padded_2(cells, sides, width):
    for axis, dim in sides:
        count = lax.axis_size(axis)
        ends = count - 1
        head = lax.slice_in_dim(cells, 0, width, axis=dim)
        tail = lax.slice_in_dim(cells, cells.shape[dim] - width, cells.shape[dim], axis=dim)
        cells = jnp.concatenate(
            [
                lax.ppermute(tail, axis, [(i, (i + 1) % count) for i in range(ends)]),
                cells,
                lax.ppermute(head, axis, [((i + 1) % count, i) for i in range(ends)]),
            ],
            axis=dim,
        )
    return cells


def from_behind(value, axis, steps):
    count = lax.axis_size(axis)
    leading, last = (max(0, -steps), min(count, count - steps))
    return lax.ppermute(value, axis, [(source, source + steps) for source in range(leading, last)])


def silu_slope(pre_act):
    sigma_val = jax.nn.sigmoid(pre_act)
    return sigma_val * (1.0 + pre_act * (1.0 - sigma_val))


def tap_views(padded, flip_sign):
    row_count = padded.shape[-3] - 2
    col_count = padded.shape[-2]
    widened = jnp.pad(padded, [(0, 0)] * (padded.ndim - 2) + [(1, 1), (0, 0)])
    pieces_list = []
    for row_off in (-1, 0, 1):
        for col_off in (-1, 0, 1):
            row_start = 1 + flip_sign * row_off
            col_start = 1 + flip_sign * col_off
            window = lax.slice_in_dim(
                widened, row_start, row_start + row_count, axis=widened.ndim - 3
            )
            window = lax.slice_in_dim(
                window, col_start, col_start + col_count, axis=widened.ndim - 2
            )
            pieces_list.append(window)
    return jnp.concatenate(pieces_list, axis=-1)


def contract_rows(left_mat, right_mat):
    return lax.dot_general(
        left_mat, right_mat, (((0,), (0,)), ((), ())), preferred_element_type=jnp.float32
    )


def contract_cols(left_mat, right_mat):
    return lax.dot_general(
        left_mat, right_mat, (((1,), (1,)), ((), ())), preferred_element_type=jnp.float32
    )


def local(
    stored_inputs, cotangent, w_reduce, w_spatial, w_expand, bias_reduce, bias_spatial, bias_expand
):
    micro_count = stored_inputs.shape[1]
    row_count = stored_inputs.shape[2]
    col_count = stored_inputs.shape[3]
    model_w = stored_inputs.shape[4]
    bottle = w_reduce.shape[2]
    pixels = row_count * col_count
    section_count = lax.axis_size("section")
    section_here = lax.axis_index("section")
    inputs_all = stored_inputs[0]
    w_one = w_reduce[0]
    w_two = w_spatial[0]
    w_three = w_expand[0]
    b_one = bias_reduce[0]
    b_two = bias_spatial[0]
    b_three = bias_expand[0]
    w_turned = w_two.reshape(9, bottle, bottle).transpose(0, 2, 1).reshape(9 * bottle, bottle)
    flat_all = inputs_all.reshape(micro_count * pixels, model_w)
    pre_one = jnp.dot(flat_all, w_one, preferred_element_type=jnp.float32) + b_one
    pre_one_all = pre_one
    act_one_all = jax.nn.silu(pre_one).astype(jnp.bfloat16)
    rims_all = padded_2(
        act_one_all.reshape(micro_count, row_count, col_count, bottle), (("tile", 1),), 1
    )
    patches = tap_views(rims_all, 1).reshape(-1, 9 * bottle)
    pre_two = jnp.dot(patches, w_two, preferred_element_type=jnp.float32) + b_two
    act_two = jax.nn.silu(pre_two).astype(jnp.bfloat16)
    pre_three = (
        jnp.dot(act_two, w_three, preferred_element_type=jnp.float32)
        + b_three
        + flat_all.astype(jnp.float32)
    )
    patches_all = patches
    pre_two_all = pre_two
    act_two_all = act_two
    pre_three_all = pre_three

    def rows_of(source, micro_id):
        return lax.dynamic_slice_in_dim(source, micro_id * pixels, pixels, 0)

    def forward_piece(micro_id):
        flat_in = lax.dynamic_index_in_dim(inputs_all, micro_id, 0, keepdims=False).reshape(
            pixels, model_w
        )
        rims = lax.dynamic_index_in_dim(rims_all, micro_id, 0, keepdims=False)
        return (
            flat_in,
            rows_of(pre_one_all, micro_id),
            rims,
            rows_of(patches_all, micro_id),
            rows_of(pre_two_all, micro_id),
            rows_of(act_two_all, micro_id),
            rows_of(pre_three_all, micro_id),
        )

    def advance(step_no, carried):
        incoming, grads_in, sum_one, sum_two, sum_three, rims_store, grad_store = carried
        micro_raw = step_no - (section_count - 1 - section_here)
        is_live = (micro_raw >= 0) & (micro_raw < micro_count)
        micro_id = jnp.clip(micro_raw, 0, micro_count - 1)
        from_loss = lax.dynamic_index_in_dim(cotangent, micro_id, 0, keepdims=False)
        upstream = jnp.where(section_here == section_count - 1, from_loss, incoming)
        flat_in, pre_one, rims, patches, pre_two, act_two, pre_three = forward_piece(micro_id)
        slope_three = upstream.reshape(pixels, model_w).astype(jnp.float32) * silu_slope(pre_three)
        grad_three = slope_three.astype(jnp.bfloat16)
        sum_three = sum_three + jnp.where(is_live, contract_rows(act_two, grad_three), 0.0)
        grad_two = (contract_cols(grad_three, w_three) * silu_slope(pre_two)).astype(jnp.bfloat16)
        sum_two = sum_two + jnp.where(is_live, contract_rows(patches, grad_two), 0.0)
        grad_rims = padded_2(grad_two.reshape(row_count, col_count, bottle), (("tile", 0),), 1)
        back_patches = tap_views(grad_rims, -1).reshape(pixels, 9 * bottle)
        spatial_back = jnp.dot(back_patches, w_turned, preferred_element_type=jnp.float32)
        grad_one = (spatial_back * silu_slope(pre_one)).astype(jnp.bfloat16)
        sum_one = sum_one + jnp.where(is_live, contract_rows(flat_in, grad_one), 0.0)
        input_grad = (contract_cols(grad_one, w_one) + slope_three).astype(jnp.bfloat16)
        input_grad = input_grad.reshape(row_count, col_count, model_w)
        grads_in = jnp.where(
            is_live,
            lax.dynamic_update_slice_in_dim(grads_in, input_grad[None], micro_id, 0),
            grads_in,
        )
        rims_store = lax.dynamic_update_slice_in_dim(rims_store, rims[None], micro_id, 0)
        incoming = from_behind(input_grad, "section", -1)
        return (incoming, grads_in, sum_one, sum_two, sum_three, rims_store, grad_store)

    start_state = (
        jnp.zeros((row_count, col_count, model_w), jnp.bfloat16),
        jnp.zeros((micro_count, row_count, col_count, model_w), jnp.bfloat16),
        jnp.zeros((model_w, bottle), jnp.float32),
        jnp.zeros((9 * bottle, bottle), jnp.float32),
        jnp.zeros((bottle, model_w), jnp.float32),
        jnp.zeros((micro_count, row_count + 2, col_count, bottle), jnp.bfloat16),
        jnp.zeros((micro_count, pixels, bottle), jnp.bfloat16),
    )
    final_state = lax.fori_loop(0, micro_count + section_count - 1, advance, start_state)
    incoming, grads_in, sum_one, sum_two, sum_three, rims_store, grad_store = final_state
    total_one, total_two, total_three = (
        lax.psum_scatter(
            sum_one.astype(jnp.bfloat16), "tile", scatter_dimension=0, tiled=True
        ).astype(jnp.float32),
        lax.psum_scatter(
            sum_two.astype(jnp.bfloat16), "tile", scatter_dimension=0, tiled=True
        ).astype(jnp.float32),
        lax.psum_scatter(
            sum_three.astype(jnp.bfloat16), "tile", scatter_dimension=0, tiled=True
        ).astype(jnp.float32),
    )
    return (grads_in[None], total_one[None], total_two[None], total_three[None])


def solution(mesh):
    return jax.shard_map(
        local,
        mesh=mesh,
        in_specs=(
            P("section", None, "tile", None, None),
            P(None, "tile", None, None),
            P("section", None, None),
            P("section", None, None),
            P("section", None, None),
            P("section", None),
            P("section", None),
            P("section", None),
        ),
        out_specs=(
            P("section", None, "tile", None, None),
            P("section", "tile", None),
            P("section", "tile", None),
            P("section", "tile", None),
        ),
        check_vma=False,
    )
```

profile of v0, /device:TPU:0, one launch (start us, length us, event | category | flops | bytes accessed | tf_op | source)
XLA Modules:
  0.0 428.4 jit_solution(2957343188634410648)
XLA Ops:
  7.2 4.3 %multiply_convert_fusion = (bf16[1536,256]{1,0:T(8,128)(2,1)S(1)}, f32[1536,256]{1,0:T(8,128)}) fusion(f32[256]{0:T(256)} %bitcast.152, bf16[1536,1024]{1,0:T(8,128)(2,1)} %bitcast.124, bf16[1,1024,256]{2,1,0:T(8,128)(2,1)} %param.12), kind=kOutput, calls=%fused_computation.55 | convolution fusion | flops 807665664 | bytes 6030336 | tf_op jit(solution)/shard_map/dot_general | solution.py:86
  12.4 2.4 collective-permute-start.3
  16.1 1.5 copy.12
  17.7 2.9 collective-permute-done.4
  23.5 3.4 broadcast_add_fusion
  28.2 3.7 convert_add_fusion
  32.9 2.1 broadcast_in_dim.70
  35.0 286.0 %while.24 = (s32[]{:T(128)}, bf16[3,128,1024]{2,1,0:T(8,128)(2,1)}, bf16[4,3,128,1024]{3,2,1,0:T(8,128)(2,1)}, f32[1024,256]{1,0:T(8,128)}, f32[2304,256]{1,0:T(...) while((s32[]{:T(128)}, bf16[3,128,1024]{2,1,0:T(8,128)(2,1)}, ...), condition=%wide.region_1.2_spmd.clone, body=%wide.region_0.1_spmd.clone.sunk | while | flops 1724479488 | bytes 59577936 | solution.py:161
  35.0 1.5 bitcast_select_fusion.2
  36.5 2.0 convert_multiply_fusion.2
  41.9 7.3 %collective-permute-start.1 = (bf16[1,128,256]{2,1,0:T(8,128)(2,1)S(1)}, bf16[1,128,256]{2,1,0:T(8,128)(2,1)S(1)}, u32[]{:S(2)}, u32[]{:S(2)}) collective-permute-start(bf16[1,128,256]{2,1,0:T(8,128)(2,1)S(1)} %get-tuple-element.655), channel_id=1, source_target_pairs={{0,1},{1,2},{2,3},{3,4},{4,5},{5,6},{6,7},{8,9},{9,10},{10,11},{11... | collective-permute-start | bytes 196616 | tf_op jit(solution)/shard_map/while/body/eval_jaxpr/ppermute | solution.py:15
  49.2 3.7 fusion.81
  54.4 1.6 fusion.79
  59.3 2.7 select_dynamic-update-slice_fusion.2
  62.9 15.3 %collective-permute-done.2 = bf16[3,128,1024]{2,1,0:T(8,128)(2,1)} collective-permute-done((bf16[3,128,1024]{2,1,0:T(8,128)(2,1)S(1)}, bf16[3,128,1024]{2,1,0:T(8,128)(2,1)}, u32[]{:S(2)}, u32[]{:S(2)}) %collective-permute-start.2) | collective-permute-done | bytes 786464 | tf_op jit(solution)/shard_map/while/body/eval_jaxpr/ppermute | solution.py:27
  78.1 1.5 bitcast_select_fusion.2
  79.6 2.0 convert_multiply_fusion.2
  85.0 3.1 collective-permute-start.1
  88.2 4.4 %fusion.81 = f32[2304,256]{1,0:T(8,128)} fusion(bf16[384,256]{1,0:T(8,128)(2,1)S(1)} %fusion.76, f32[2304,256]{1,0:T(8,128)} %get-tuple-element.694, bf16[1536,2304]{1,0:T(8,128)(2,1)} %get-tuple-element.730, s32[]{:T(128)S(6)} %select_n.180, pred[]{:T(512)S(6)} %compare.89, pred[]{:T(512)S(6)} %and.51), kind=kOutput, calls=%fused_computation.1.clone.1 | convolution fusion | flops 454754304 | bytes 6684678 | tf_op jit(solution)/shard_map/while/body/eval_jaxpr/dot_general | solution.py:55
  94.2 1.6 fusion.79
  99.0 2.7 select_dynamic-update-slice_fusion.2
  102.6 15.4 %collective-permute-done.2 = bf16[3,128,1024]{2,1,0:T(8,128)(2,1)} collective-permute-done((bf16[3,128,1024]{2,1,0:T(8,128)(2,1)S(1)}, bf16[3,128,1024]{2,1,0:T(8,128)(2,1)}, u32[]{:S(2)}, u32[]{:S(2)}) %collective-permute-start.2) | collective-permute-done | bytes 786464 | tf_op jit(solution)/shard_map/while/body/eval_jaxpr/ppermute | solution.py:27
  118.0 1.5 bitcast_select_fusion.2
  119.4 2.0 convert_multiply_fusion.2
  124.8 3.4 collective-permute-start.1
  128.3 4.4 %fusion.81 = f32[2304,256]{1,0:T(8,128)} fusion(bf16[384,256]{1,0:T(8,128)(2,1)S(1)} %fusion.76, f32[2304,256]{1,0:T(8,128)} %get-tuple-element.694, bf16[1536,2304]{1,0:T(8,128)(2,1)} %get-tuple-element.730, s32[]{:T(128)S(6)} %select_n.180, pred[]{:T(512)S(6)} %compare.89, pred[]{:T(512)S(6)} %and.51), kind=kOutput, calls=%fused_computation.1.clone.1 | convolution fusion | flops 454754304 | bytes 6684678 | tf_op jit(solution)/shard_map/while/body/eval_jaxpr/dot_general | solution.py:55
  134.2 1.6 fusion.79
  139.1 2.7 select_dynamic-update-slice_fusion.2
  142.7 15.9 %collective-permute-done.2 = bf16[3,128,1024]{2,1,0:T(8,128)(2,1)} collective-permute-done((bf16[3,128,1024]{2,1,0:T(8,128)(2,1)S(1)}, bf16[3,128,1024]{2,1,0:T(8,128)(2,1)}, u32[]{:S(2)}, u32[]{:S(2)}) %collective-permute-start.2) | collective-permute-done | bytes 786464 | tf_op jit(solution)/shard_map/while/body/eval_jaxpr/ppermute | solution.py:27
  158.6 1.5 bitcast_select_fusion.2
  160.0 2.0 convert_multiply_fusion.2
  165.4 3.4 collective-permute-start.1
  168.9 4.4 %fusion.81 = f32[2304,256]{1,0:T(8,128)} fusion(bf16[384,256]{1,0:T(8,128)(2,1)S(1)} %fusion.76, f32[2304,256]{1,0:T(8,128)} %get-tuple-element.694, bf16[1536,2304]{1,0:T(8,128)(2,1)} %get-tuple-element.730, s32[]{:T(128)S(6)} %select_n.180, pred[]{:T(512)S(6)} %compare.89, pred[]{:T(512)S(6)} %and.51), kind=kOutput, calls=%fused_computation.1.clone.1 | convolution fusion | flops 454754304 | bytes 6684678 | tf_op jit(solution)/shard_map/while/body/eval_jaxpr/dot_general | solution.py:55
  174.8 1.6 fusion.79
  179.7 2.7 select_dynamic-update-slice_fusion.2
  183.3 15.9 %collective-permute-done.2 = bf16[3,128,1024]{2,1,0:T(8,128)(2,1)} collective-permute-done((bf16[3,128,1024]{2,1,0:T(8,128)(2,1)S(1)}, bf16[3,128,1024]{2,1,0:T(8,128)(2,1)}, u32[]{:S(2)}, u32[]{:S(2)}) %collective-permute-start.2) | collective-permute-done | bytes 786464 | tf_op jit(solution)/shard_map/while/body/eval_jaxpr/ppermute | solution.py:27
  199.2 1.5 bitcast_select_fusion.2
  200.6 2.0 convert_multiply_fusion.2
  206.1 3.4 collective-permute-start.1
  209.5 4.4 %fusion.81 = f32[2304,256]{1,0:T(8,128)} fusion(bf16[384,256]{1,0:T(8,128)(2,1)S(1)} %fusion.76, f32[2304,256]{1,0:T(8,128)} %get-tuple-element.694, bf16[1536,2304]{1,0:T(8,128)(2,1)} %get-tuple-element.730, s32[]{:T(128)S(6)} %select_n.180, pred[]{:T(512)S(6)} %compare.89, pred[]{:T(512)S(6)} %and.51), kind=kOutput, calls=%fused_computation.1.clone.1 | convolution fusion | flops 454754304 | bytes 6684678 | tf_op jit(solution)/shard_map/while/body/eval_jaxpr/dot_general | solution.py:55
  215.5 1.6 fusion.79
  220.3 2.7 select_dynamic-update-slice_fusion.2
  223.9 15.9 %collective-permute-done.2 = bf16[3,128,1024]{2,1,0:T(8,128)(2,1)} collective-permute-done((bf16[3,128,1024]{2,1,0:T(8,128)(2,1)S(1)}, bf16[3,128,1024]{2,1,0:T(8,128)(2,1)}, u32[]{:S(2)}, u32[]{:S(2)}) %collective-permute-start.2) | collective-permute-done | bytes 786464 | tf_op jit(solution)/shard_map/while/body/eval_jaxpr/ppermute | solution.py:27
  239.8 1.5 bitcast_select_fusion.2
  241.2 2.0 convert_multiply_fusion.2
  246.7 3.4 collective-permute-start.1
  250.1 4.4 %fusion.81 = f32[2304,256]{1,0:T(8,128)} fusion(bf16[384,256]{1,0:T(8,128)(2,1)S(1)} %fusion.76, f32[2304,256]{1,0:T(8,128)} %get-tuple-element.694, bf16[1536,2304]{1,0:T(8,128)(2,1)} %get-tuple-element.730, s32[]{:T(128)S(6)} %select_n.180, pred[]{:T(512)S(6)} %compare.89, pred[]{:T(512)S(6)} %and.51), kind=kOutput, calls=%fused_computation.1.clone.1 | convolution fusion | flops 454754304 | bytes 6684678 | tf_op jit(solution)/shard_map/while/body/eval_jaxpr/dot_general | solution.py:55
  256.1 1.6 fusion.79
  260.9 2.7 select_dynamic-update-slice_fusion.2
  264.5 15.9 %collective-permute-done.2 = bf16[3,128,1024]{2,1,0:T(8,128)(2,1)} collective-permute-done((bf16[3,128,1024]{2,1,0:T(8,128)(2,1)S(1)}, bf16[3,128,1024]{2,1,0:T(8,128)(2,1)}, u32[]{:S(2)}, u32[]{:S(2)}) %collective-permute-start.2) | collective-permute-done | bytes 786464 | tf_op jit(solution)/shard_map/while/body/eval_jaxpr/ppermute | solution.py:27
  280.4 1.5 bitcast_select_fusion.2
  281.9 2.0 convert_multiply_fusion.2
  287.3 3.4 collective-permute-start.1
  290.7 4.4 %fusion.81 = f32[2304,256]{1,0:T(8,128)} fusion(bf16[384,256]{1,0:T(8,128)(2,1)S(1)} %fusion.76, f32[2304,256]{1,0:T(8,128)} %get-tuple-element.694, bf16[1536,2304]{1,0:T(8,128)(2,1)} %get-tuple-element.730, s32[]{:T(128)S(6)} %select_n.180, pred[]{:T(512)S(6)} %compare.89, pred[]{:T(512)S(6)} %and.51), kind=kOutput, calls=%fused_computation.1.clone.1 | convolution fusion | flops 454754304 | bytes 6684678 | tf_op jit(solution)/shard_map/while/body/eval_jaxpr/dot_general | solution.py:55
  296.7 1.6 fusion.79
  301.5 2.7 select_dynamic-update-slice_fusion.2
  305.1 15.9 %collective-permute-done.2 = bf16[3,128,1024]{2,1,0:T(8,128)(2,1)} collective-permute-done((bf16[3,128,1024]{2,1,0:T(8,128)(2,1)S(1)}, bf16[3,128,1024]{2,1,0:T(8,128)(2,1)}, u32[]{:S(2)}, u32[]{:S(2)}) %collective-permute-start.2) | collective-permute-done | bytes 786464 | tf_op jit(solution)/shard_map/while/body/eval_jaxpr/ppermute | solution.py:27
  321.9 2.1 convert_element_type.87
  325.3 29.4 %reduce-scatter.8.cloned.1.call-done = bf16[32,1024]{1,0:T(8,128)(2,1)} async-done(((bf16[256,1024]{1,0:T(8,128)(2,1)}), bf16[32,1024]{1,0:T(8,128)(2,1)}) %reduce-scatter.8.cloned.1.call-update) | async-done | bytes 65552 | tf_op jit(solution)/shard_map/reduce_scatter | solution.py:170
  354.7 1.5 bitcast_convert_fusion.1
  356.2 30.4 %reduce-scatter.4.cloned.1.call-done = bf16[128,256]{1,0:T(8,128)(2,1)} async-done(((bf16[1024,256]{1,0:T(8,128)(2,1)}), bf16[128,256]{1,0:T(8,128)(2,1)}) %reduce-scatter.4.cloned.1.call-update) | async-done | bytes 65552 | tf_op jit(solution)/shard_map/reduce_scatter | solution.py:164
  386.6 1.5 bitcast_convert_fusion.2
  388.1 32.2 %reduce-scatter.6.cloned.1.call-done = bf16[288,256]{1,0:T(8,128)(2,1)} async-done(((bf16[2304,256]{1,0:T(8,128)(2,1)}), bf16[288,256]{1,0:T(8,128)(2,1)}) %reduce-scatter.6.cloned.1.call-update) | async-done | bytes 147472 | tf_op jit(solution)/shard_map/reduce_scatter | solution.py:167
  420.2 1.6 bitcast_convert_fusion
  (248 shorter events, 71.5 us)
Async XLA Ops:
  7.2 347.5 %reduce-scatter.8.cloned.1.call-start = ((), (), s32[]{:S(2)}) async-start(), calls=%async_computation.5 | async-start | bytes 589824 | tf_op jit(solution)/shard_map/reduce_scatter | solution.py:170
  7.2 8.9 %copy-start.7 = (bf16[1,2304,256]{2,1,0:T(8,128)(2,1)S(1)}, bf16[1,2304,256]{2,1,0:T(8,128)(2,1)}, u32[]{:S(2)}) copy-start(bf16[1,2304,256]{2,1,0:T(8,128)(2,1)} %param.13) | copy-start | bytes 3538948
  12.4 5.3 %collective-permute-start.3 = (bf16[4,1,128,256]{3,2,1,0:T(8,128)(2,1)}, bf16[4,1,128,256]{3,2,1,0:T(8,128)(2,1)S(1)}, u32[]{:S(2)}, u32[]{:S(2)}) collective-permute-start(bf16[4,1,128,256]{3,2,1,0:T(8,128)(2,1)} %get-tuple-element.529), channel_id=1, source_target_pairs={{0,1},{1,2},{2,3},{3,4},{4,5},{5,6},{6,7},{8,9},{9,10},{10,11},{11... | collective-permute-start | bytes 786440 | tf_op jit(solution)/shard_map/ppermute | solution.py:15
  14.8 5.8 %collective-permute-start.4 = (bf16[4,1,128,256]{3,2,1,0:T(8,128)(2,1)}, bf16[4,1,128,256]{3,2,1,0:T(8,128)(2,1)S(1)}, u32[]{:S(2)}, u32[]{:S(2)}) collective-permute-start(bf16[4,1,128,256]{3,2,1,0:T(8,128)(2,1)} %get-tuple-element.530), channel_id=1, source_target_pairs={{1,0},{2,1},{3,2},{4,3},{5,4},{6,5},{7,6},{9,8},{10,9},{11,10},{12... | collective-permute-start | bytes 786440 | tf_op jit(solution)/shard_map/ppermute | solution.py:17
  22.9 0.7 copy-start.12
  23.0 4.1 copy-start.4
  23.5 4.2 copy-start.3
  23.5 4.7 %copy-start.9 = (bf16[1,256,1024]{2,1,0:T(8,128)(2,1)S(1)}, bf16[1,256,1024]{2,1,0:T(8,128)(2,1)}, u32[]{:S(2)}) copy-start(bf16[1,256,1024]{2,1,0:T(8,128)(2,1)} %param.14) | copy-start | bytes 1572868
  23.5 4.7 %copy-start.11 = (f32[1,1024]{1,0:T(1,128)S(1)}, f32[1,1024]{1,0:T(1,128)}, u32[]{:S(2)}) copy-start(f32[1,1024]{1,0:T(1,128)} %param.17) | copy-start | bytes 12292
  27.1 4.9 %copy-start.6 = (bf16[1536,256]{1,0:T(8,128)(2,1)}, bf16[1536,256]{1,0:T(8,128)(2,1)S(1)}, u32[]{:S(2)}) copy-start(bf16[1536,256]{1,0:T(8,128)(2,1)S(1)} %get-tuple-element.683) | copy-start | bytes 2359300
  32.9 2.1 copy-start.5
  36.4 2.1 copy-start.10
  40.6 12.3 %collective-permute-start = (bf16[1,128,256]{2,1,0:T(8,128)(2,1)}, bf16[1,128,256]{2,1,0:T(8,128)(2,1)S(1)}, u32[]{:S(2)}, u32[]{:S(2)}) collective-permute-start(bf16[1,128,256]{2,1,0:T(8,128)(2,1)} %get-tuple-element.654), channel_id=1, source_target_pairs={{1,0},{2,1},{3,2},{4,3},{5,4},{6,5},{7,6},{9,8},{10,9},{11,10},{12... | collective-permute-start | bytes 196616 | tf_op jit(solution)/shard_map/while/body/eval_jaxpr/ppermute | solution.py:17
  41.9 11.0 %collective-permute-start.1 = (bf16[1,128,256]{2,1,0:T(8,128)(2,1)S(1)}, bf16[1,128,256]{2,1,0:T(8,128)(2,1)S(1)}, u32[]{:S(2)}, u32[]{:S(2)}) collective-permute-start(bf16[1,128,256]{2,1,0:T(8,128)(2,1)S(1)} %get-tuple-element.655), channel_id=1, source_target_pairs={{0,1},{1,2},{2,3},{3,4},{4,5},{5,6},{6,7},{8,9},{9,10},{10,11},{11... | collective-permute-start | bytes 196616 | tf_op jit(solution)/shard_map/while/body/eval_jaxpr/ppermute | solution.py:15
  53.2 1.3 copy-start.8
  56.5 21.7 %collective-permute-start.2 = (bf16[3,128,1024]{2,1,0:T(8,128)(2,1)S(1)}, bf16[3,128,1024]{2,1,0:T(8,128)(2,1)}, u32[]{:S(2)}, u32[]{:S(2)}) collective-permute-start(bf16[3,128,1024]{2,1,0:T(8,128)(2,1)S(1)} %bitcast.121), channel_id=1, source_target_pairs={{8,0},{16,8},{24,16},{9,1},{17,9},{25,17},{10,2},{18,10},{26,18},{... | collective-permute-start | bytes 2359304 | tf_op jit(solution)/shard_map/while/body/eval_jaxpr/ppermute | solution.py:27
  59.2 2.7 copy-start.1
  62.9 15.3 %copy-start.2 = (f32[1024,256]{1,0:T(8,128)}, f32[1024,256]{1,0:T(8,128)S(1)}, u32[]{:S(2)}) copy-start(f32[1024,256]{1,0:T(8,128)S(1)} %fusion.80) | copy-start | bytes 3145732 | tf_op jit(solution)/shard_map/while
  79.6 2.1 copy-start.10
  83.7 8.9 %collective-permute-start = (bf16[1,128,256]{2,1,0:T(8,128)(2,1)}, bf16[1,128,256]{2,1,0:T(8,128)(2,1)S(1)}, u32[]{:S(2)}, u32[]{:S(2)}) collective-permute-start(bf16[1,128,256]{2,1,0:T(8,128)(2,1)} %get-tuple-element.654), channel_id=1, source_target_pairs={{1,0},{2,1},{3,2},{4,3},{5,4},{6,5},{7,6},{9,8},{10,9},{11,10},{12... | collective-permute-start | bytes 196616 | tf_op jit(solution)/shard_map/while/body/eval_jaxpr/ppermute | solution.py:17
  85.0 7.6 %collective-permute-start.1 = (bf16[1,128,256]{2,1,0:T(8,128)(2,1)S(1)}, bf16[1,128,256]{2,1,0:T(8,128)(2,1)S(1)}, u32[]{:S(2)}, u32[]{:S(2)}) collective-permute-start(bf16[1,128,256]{2,1,0:T(8,128)(2,1)S(1)} %get-tuple-element.655), channel_id=1, source_target_pairs={{0,1},{1,2},{2,3},{3,4},{4,5},{5,6},{6,7},{8,9},{9,10},{10,11},{11... | collective-permute-start | bytes 196616 | tf_op jit(solution)/shard_map/while/body/eval_jaxpr/ppermute | solution.py:15
  92.9 1.3 copy-start.8
  96.2 21.8 %collective-permute-start.2 = (bf16[3,128,1024]{2,1,0:T(8,128)(2,1)S(1)}, bf16[3,128,1024]{2,1,0:T(8,128)(2,1)}, u32[]{:S(2)}, u32[]{:S(2)}) collective-permute-start(bf16[3,128,1024]{2,1,0:T(8,128)(2,1)S(1)} %bitcast.121), channel_id=1, source_target_pairs={{8,0},{16,8},{24,16},{9,1},{17,9},{25,17},{10,2},{18,10},{26,18},{... | collective-permute-start | bytes 2359304 | tf_op jit(solution)/shard_map/while/body/eval_jaxpr/ppermute | solution.py:27
  99.0 2.7 copy-start.1
  102.6 15.4 %copy-start.2 = (f32[1024,256]{1,0:T(8,128)}, f32[1024,256]{1,0:T(8,128)S(1)}, u32[]{:S(2)}) copy-start(f32[1024,256]{1,0:T(8,128)S(1)} %fusion.80) | copy-start | bytes 3145732 | tf_op jit(solution)/shard_map/while
  119.4 2.1 copy-start.10
  123.5 9.1 %collective-permute-start = (bf16[1,128,256]{2,1,0:T(8,128)(2,1)}, bf16[1,128,256]{2,1,0:T(8,128)(2,1)S(1)}, u32[]{:S(2)}, u32[]{:S(2)}) collective-permute-start(bf16[1,128,256]{2,1,0:T(8,128)(2,1)} %get-tuple-element.654), channel_id=1, source_target_pairs={{1,0},{2,1},{3,2},{4,3},{5,4},{6,5},{7,6},{9,8},{10,9},{11,10},{12... | collective-permute-start | bytes 196616 | tf_op jit(solution)/shard_map/while/body/eval_jaxpr/ppermute | solution.py:17
  124.8 7.9 %collective-permute-start.1 = (bf16[1,128,256]{2,1,0:T(8,128)(2,1)S(1)}, bf16[1,128,256]{2,1,0:T(8,128)(2,1)S(1)}, u32[]{:S(2)}, u32[]{:S(2)}) collective-permute-start(bf16[1,128,256]{2,1,0:T(8,128)(2,1)S(1)} %get-tuple-element.655), channel_id=1, source_target_pairs={{0,1},{1,2},{2,3},{3,4},{4,5},{5,6},{6,7},{8,9},{9,10},{10,11},{11... | collective-permute-start | bytes 196616 | tf_op jit(solution)/shard_map/while/body/eval_jaxpr/ppermute | solution.py:15
  133.0 1.3 copy-start.8
  136.3 22.3 %collective-permute-start.2 = (bf16[3,128,1024]{2,1,0:T(8,128)(2,1)S(1)}, bf16[3,128,1024]{2,1,0:T(8,128)(2,1)}, u32[]{:S(2)}, u32[]{:S(2)}) collective-permute-start(bf16[3,128,1024]{2,1,0:T(8,128)(2,1)S(1)} %bitcast.121), channel_id=1, source_target_pairs={{8,0},{16,8},{24,16},{9,1},{17,9},{25,17},{10,2},{18,10},{26,18},{... | collective-permute-start | bytes 2359304 | tf_op jit(solution)/shard_map/while/body/eval_jaxpr/ppermute | solution.py:27
  139.0 2.7 copy-start.1
  142.7 15.9 %copy-start.2 = (f32[1024,256]{1,0:T(8,128)}, f32[1024,256]{1,0:T(8,128)S(1)}, u32[]{:S(2)}) copy-start(f32[1024,256]{1,0:T(8,128)S(1)} %fusion.80) | copy-start | bytes 3145732 | tf_op jit(solution)/shard_map/while
  160.0 2.1 copy-start.10
  164.2 9.1 %collective-permute-start = (bf16[1,128,256]{2,1,0:T(8,128)(2,1)}, bf16[1,128,256]{2,1,0:T(8,128)(2,1)S(1)}, u32[]{:S(2)}, u32[]{:S(2)}) collective-permute-start(bf16[1,128,256]{2,1,0:T(8,128)(2,1)} %get-tuple-element.654), channel_id=1, source_target_pairs={{1,0},{2,1},{3,2},{4,3},{5,4},{6,5},{7,6},{9,8},{10,9},{11,10},{12... | collective-permute-start | bytes 196616 | tf_op jit(solution)/shard_map/while/body/eval_jaxpr/ppermute | solution.py:17
  165.4 7.9 %collective-permute-start.1 = (bf16[1,128,256]{2,1,0:T(8,128)(2,1)S(1)}, bf16[1,128,256]{2,1,0:T(8,128)(2,1)S(1)}, u32[]{:S(2)}, u32[]{:S(2)}) collective-permute-start(bf16[1,128,256]{2,1,0:T(8,128)(2,1)S(1)} %get-tuple-element.655), channel_id=1, source_target_pairs={{0,1},{1,2},{2,3},{3,4},{4,5},{5,6},{6,7},{8,9},{9,10},{10,11},{11... | collective-permute-start | bytes 196616 | tf_op jit(solution)/shard_map/while/body/eval_jaxpr/ppermute | solution.py:15
  173.6 1.3 copy-start.8
  176.9 22.3 %collective-permute-start.2 = (bf16[3,128,1024]{2,1,0:T(8,128)(2,1)S(1)}, bf16[3,128,1024]{2,1,0:T(8,128)(2,1)}, u32[]{:S(2)}, u32[]{:S(2)}) collective-permute-start(bf16[3,128,1024]{2,1,0:T(8,128)(2,1)S(1)} %bitcast.121), channel_id=1, source_target_pairs={{8,0},{16,8},{24,16},{9,1},{17,9},{25,17},{10,2},{18,10},{26,18},{... | collective-permute-start | bytes 2359304 | tf_op jit(solution)/shard_map/while/body/eval_jaxpr/ppermute | solution.py:27
  179.6 2.7 copy-start.1
  183.3 15.9 %copy-start.2 = (f32[1024,256]{1,0:T(8,128)}, f32[1024,256]{1,0:T(8,128)S(1)}, u32[]{:S(2)}) copy-start(f32[1024,256]{1,0:T(8,128)S(1)} %fusion.80) | copy-start | bytes 3145732 | tf_op jit(solution)/shard_map/while
  200.6 2.1 copy-start.10
  204.8 9.1 %collective-permute-start = (bf16[1,128,256]{2,1,0:T(8,128)(2,1)}, bf16[1,128,256]{2,1,0:T(8,128)(2,1)S(1)}, u32[]{:S(2)}, u32[]{:S(2)}) collective-permute-start(bf16[1,128,256]{2,1,0:T(8,128)(2,1)} %get-tuple-element.654), channel_id=1, source_target_pairs={{1,0},{2,1},{3,2},{4,3},{5,4},{6,5},{7,6},{9,8},{10,9},{11,10},{12... | collective-permute-start | bytes 196616 | tf_op jit(solution)/shard_map/while/body/eval_jaxpr/ppermute | solution.py:17
  206.1 7.9 %collective-permute-start.1 = (bf16[1,128,256]{2,1,0:T(8,128)(2,1)S(1)}, bf16[1,128,256]{2,1,0:T(8,128)(2,1)S(1)}, u32[]{:S(2)}, u32[]{:S(2)}) collective-permute-start(bf16[1,128,256]{2,1,0:T(8,128)(2,1)S(1)} %get-tuple-element.655), channel_id=1, source_target_pairs={{0,1},{1,2},{2,3},{3,4},{4,5},{5,6},{6,7},{8,9},{9,10},{10,11},{11... | collective-permute-start | bytes 196616 | tf_op jit(solution)/shard_map/while/body/eval_jaxpr/ppermute | solution.py:15
  214.2 1.3 copy-start.8
  217.5 22.3 %collective-permute-start.2 = (bf16[3,128,1024]{2,1,0:T(8,128)(2,1)S(1)}, bf16[3,128,1024]{2,1,0:T(8,128)(2,1)}, u32[]{:S(2)}, u32[]{:S(2)}) collective-permute-start(bf16[3,128,1024]{2,1,0:T(8,128)(2,1)S(1)} %bitcast.121), channel_id=1, source_target_pairs={{8,0},{16,8},{24,16},{9,1},{17,9},{25,17},{10,2},{18,10},{26,18},{... | collective-permute-start | bytes 2359304 | tf_op jit(solution)/shard_map/while/body/eval_jaxpr/ppermute | solution.py:27
  220.3 2.7 copy-start.1
  223.9 15.9 %copy-start.2 = (f32[1024,256]{1,0:T(8,128)}, f32[1024,256]{1,0:T(8,128)S(1)}, u32[]{:S(2)}) copy-start(f32[1024,256]{1,0:T(8,128)S(1)} %fusion.80) | copy-start | bytes 3145732 | tf_op jit(solution)/shard_map/while
  241.2 2.1 copy-start.10
  245.4 9.1 %collective-permute-start = (bf16[1,128,256]{2,1,0:T(8,128)(2,1)}, bf16[1,128,256]{2,1,0:T(8,128)(2,1)S(1)}, u32[]{:S(2)}, u32[]{:S(2)}) collective-permute-start(bf16[1,128,256]{2,1,0:T(8,128)(2,1)} %get-tuple-element.654), channel_id=1, source_target_pairs={{1,0},{2,1},{3,2},{4,3},{5,4},{6,5},{7,6},{9,8},{10,9},{11,10},{12... | collective-permute-start | bytes 196616 | tf_op jit(solution)/shard_map/while/body/eval_jaxpr/ppermute | solution.py:17
  246.7 7.9 %collective-permute-start.1 = (bf16[1,128,256]{2,1,0:T(8,128)(2,1)S(1)}, bf16[1,128,256]{2,1,0:T(8,128)(2,1)S(1)}, u32[]{:S(2)}, u32[]{:S(2)}) collective-permute-start(bf16[1,128,256]{2,1,0:T(8,128)(2,1)S(1)} %get-tuple-element.655), channel_id=1, source_target_pairs={{0,1},{1,2},{2,3},{3,4},{4,5},{5,6},{6,7},{8,9},{9,10},{10,11},{11... | collective-permute-start | bytes 196616 | tf_op jit(solution)/shard_map/while/body/eval_jaxpr/ppermute | solution.py:15
  254.8 1.3 copy-start.8
  258.1 22.3 %collective-permute-start.2 = (bf16[3,128,1024]{2,1,0:T(8,128)(2,1)S(1)}, bf16[3,128,1024]{2,1,0:T(8,128)(2,1)}, u32[]{:S(2)}, u32[]{:S(2)}) collective-permute-start(bf16[3,128,1024]{2,1,0:T(8,128)(2,1)S(1)} %bitcast.121), channel_id=1, source_target_pairs={{8,0},{16,8},{24,16},{9,1},{17,9},{25,17},{10,2},{18,10},{26,18},{... | collective-permute-start | bytes 2359304 | tf_op jit(solution)/shard_map/while/body/eval_jaxpr/ppermute | solution.py:27
  260.9 2.7 copy-start.1
  264.5 15.9 %copy-start.2 = (f32[1024,256]{1,0:T(8,128)}, f32[1024,256]{1,0:T(8,128)S(1)}, u32[]{:S(2)}) copy-start(f32[1024,256]{1,0:T(8,128)S(1)} %fusion.80) | copy-start | bytes 3145732 | tf_op jit(solution)/shard_map/while
  281.8 2.1 copy-start.10
  286.0 9.1 %collective-permute-start = (bf16[1,128,256]{2,1,0:T(8,128)(2,1)}, bf16[1,128,256]{2,1,0:T(8,128)(2,1)S(1)}, u32[]{:S(2)}, u32[]{:S(2)}) collective-permute-start(bf16[1,128,256]{2,1,0:T(8,128)(2,1)} %get-tuple-element.654), channel_id=1, source_target_pairs={{1,0},{2,1},{3,2},{4,3},{5,4},{6,5},{7,6},{9,8},{10,9},{11,10},{12... | collective-permute-start | bytes 196616 | tf_op jit(solution)/shard_map/while/body/eval_jaxpr/ppermute | solution.py:17
  287.3 7.9 %collective-permute-start.1 = (bf16[1,128,256]{2,1,0:T(8,128)(2,1)S(1)}, bf16[1,128,256]{2,1,0:T(8,128)(2,1)S(1)}, u32[]{:S(2)}, u32[]{:S(2)}) collective-permute-start(bf16[1,128,256]{2,1,0:T(8,128)(2,1)S(1)} %get-tuple-element.655), channel_id=1, source_target_pairs={{0,1},{1,2},{2,3},{3,4},{4,5},{5,6},{6,7},{8,9},{9,10},{10,11},{11... | collective-permute-start | bytes 196616 | tf_op jit(solution)/shard_map/while/body/eval_jaxpr/ppermute | solution.py:15
  295.4 1.3 copy-start.8
  298.7 22.3 %collective-permute-start.2 = (bf16[3,128,1024]{2,1,0:T(8,128)(2,1)S(1)}, bf16[3,128,1024]{2,1,0:T(8,128)(2,1)}, u32[]{:S(2)}, u32[]{:S(2)}) collective-permute-start(bf16[3,128,1024]{2,1,0:T(8,128)(2,1)S(1)} %bitcast.121), channel_id=1, source_target_pairs={{8,0},{16,8},{24,16},{9,1},{17,9},{25,17},{10,2},{18,10},{26,18},{... | collective-permute-start | bytes 2359304 | tf_op jit(solution)/shard_map/while/body/eval_jaxpr/ppermute | solution.py:27
  301.5 2.7 copy-start.1
  305.1 15.9 %copy-start.2 = (f32[1024,256]{1,0:T(8,128)}, f32[1024,256]{1,0:T(8,128)S(1)}, u32[]{:S(2)}) copy-start(f32[1024,256]{1,0:T(8,128)S(1)} %fusion.80) | copy-start | bytes 3145732 | tf_op jit(solution)/shard_map/while
  321.0 3.1 copy-start
  321.9 64.7 %reduce-scatter.4.cloned.1.call-start = ((), (), s32[]{:S(2)}) async-start(), calls=%async_computation.3 | async-start | bytes 589824 | tf_op jit(solution)/shard_map/reduce_scatter | solution.py:164
  324.1 96.2 %reduce-scatter.6.cloned.1.call-start = ((), (), s32[]{:S(2)}) async-start(), calls=%async_computation.4 | async-start | bytes 1327104 | tf_op jit(solution)/shard_map/reduce_scatter | solution.py:167
Sparse Core Ops, SparseCore 0:
  322.0 32.6 reduce-scatter.7
  356.9 29.5 reduce-scatter.3
  388.9 31.3 reduce-scatter.5
where the time goes:
time: 431 us; the launch traced here: 428 us
  waiting for transfers between devices  205 us (48%)
  matrix products  82.5 us (19%)
  other arithmetic  53.7 us (12%)
  starting transfers between devices  49.2 us (11%)
  local copies, waits for them, and re-layouts  22.5 us (5%)
  between operations  13.9 us (3%)
    ppermute x7, waiting for transfers between devices, from_behind(): lax.ppermute(value, axis, [(source, source + steps) for source in range(l...  110 us
    dot_general x21, matrix products, contract_rows(): lax.dot_general(left_mat, right_mat, (((0,), (0,)), ((), ())), preferred_...  46.9 us
    reduce_scatter x1, waiting for transfers between devices, local(): lax.psum_scatter(sum_two.astype(jnp.bfloat16), 'tile', scatter_dimension=...  32.2 us
    reduce_scatter x1, waiting for transfers between devices, local(): lax.psum_scatter(sum_one.astype(jnp.bfloat16), 'tile', scatter_dimension=...  30.4 us
    ppermute x8, starting transfers between devices, padded_2(): lax.ppermute(tail, axis, [(i, (i + 1) % count) for i in range(ends)])  29.8 us
    reduce_scatter x1, waiting for transfers between devices, local(): lax.psum_scatter(sum_three.astype(jnp.bfloat16), 'tile', scatter_dimensio...  29.4 us
    select_n x7, other arithmetic, advance(): jnp.where(is_live, lax.dynamic_update_slice_in_dim(grads_in, input_grad[N...  18.8 us
    mul x7, other arithmetic, advance(): upstream.reshape(pixels, model_w).astype(jnp.float32)  14.3 us
  transfers between devices with their start and end apart: 26, of which 11 were waited for; matrix products, arithmetic and copies ran while one was open for 17% of the time, Pallas kernels for 0%

commit v1 on v0

v1 whole, which is shorter than its diff:
```python
import functools

import jax
import jax.numpy as jnp
from jax import lax
from jax.experimental import pallas as pl
from jax.experimental.pallas import tpu as pltpu
from jax.sharding import PartitionSpec as P

BF = jnp.bfloat16
F32 = jnp.float32
PAD = 8
PIECES = 4


def silu_and_slope(pre_act):
    sigma_val = jax.nn.sigmoid(pre_act)
    return pre_act * sigma_val, sigma_val * (1.0 + pre_act * (1.0 - sigma_val))


def dot_nn(left, right):
    return jnp.dot(left, right, preferred_element_type=F32)


def dot_nt(left, right):
    return lax.dot_general(left, right, (((1,), (1,)), ((), ())), preferred_element_type=F32)


def dot_tn(left, right):
    return lax.dot_general(left, right, (((0,), (0,)), ((), ())), preferred_element_type=F32)


def kernel(
    sections, tiles, x_ref, cot_ref, w1_ref, w2_ref, w3_ref, b1_ref, b2_ref, b3_ref,
    gin_ref, o1_ref, o2_ref, o3_ref,
    up, slope1, slope2, slope3, act_pad, taps, act2, g_pad, g3, g1,
    fe_out, fe_in, be_out, be_in, sum1, sum2, sum3,
    p1, p2, p3, q1, q2, q3, r1, r2, r3, s1, s2, s3,
    cot_sem, up_ss, up_rs, fe_ss, fe_rs, be_ss, be_rs, a_ss, a_rs, z_ss, z_rs,
):
    micros, rows, cols, model = x_ref.shape
    bottle = w1_ref.shape[1]
    pixels = rows * cols
    width = cols // PIECES
    half = tiles // 2
    sec = lax.axis_index("section")
    tile = lax.axis_index("tile")
    core = lax.rem(tile, 2)
    zed = tile // 2
    is_last = sec == sections - 1
    has_above = tile > 0
    has_below = tile < tiles - 1
    partner = tile + 1 - 2 * core

    barrier = pltpu.get_barrier_semaphore()

    def greet(cond, target):
        @pl.when(cond)
        def _():
            pl.semaphore_signal(barrier, inc=1, device_id=target, device_id_type=pl.DeviceIdType.MESH)

    greet(has_above, {"tile": tile - 1})
    greet(has_below, {"tile": tile + 1})
    greet(sec > 0, {"section": sec - 1})
    greet(sec < sections - 1, {"section": sec + 1})
    for step in range(1, half):
        other = lax.rem(zed + step, half) * 2 + core
        pl.semaphore_signal(barrier, inc=1, device_id={"tile": other}, device_id_type=pl.DeviceIdType.MESH)

    def cot_copy(m):
        return pltpu.make_async_copy(cot_ref.at[m], up.at[m], cot_sem.at[m])

    @pl.when(is_last)
    def _():
        for m in range(micros):
            cot_copy(m).start()

    act_pad[...] = jnp.zeros(act_pad.shape, F32)
    g_pad[...] = jnp.zeros(g_pad.shape, F32)
    sum1[...] = jnp.zeros(sum1.shape, F32)
    sum2[...] = jnp.zeros(sum2.shape, F32)
    sum3[...] = jnp.zeros(sum3.shape, F32)

    def remote(src, dst, ss, rs, target):
        return pltpu.make_async_remote_copy(
            src_ref=src, dst_ref=dst, send_sem=ss, recv_sem=rs,
            device_id=target, device_id_type=pl.DeviceIdType.MESH,
        )

    def fe_up(m):
        return remote(fe_out.at[m, 0], fe_in.at[m, 1], fe_ss.at[m, 0], fe_rs.at[m, 1], {"tile": tile - 1})

    def fe_down(m):
        return remote(fe_out.at[m, 1], fe_in.at[m, 0], fe_ss.at[m, 1], fe_rs.at[m, 0], {"tile": tile + 1})

    def cut(j):
        return pl.ds(j * width, width)

    def be_up(m, j):
        n = m * PIECES + j
        return remote(
            be_out.at[m, 0, cut(j)], be_in.at[m, 1, cut(j)], be_ss.at[n, 0], be_rs.at[n, 1],
            {"tile": tile - 1},
        )

    def be_down(m, j):
        n = m * PIECES + j
        return remote(
            be_out.at[m, 1, cut(j)], be_in.at[m, 0, cut(j)], be_ss.at[n, 1], be_rs.at[n, 0],
            {"tile": tile + 1},
        )

    def relay(m, j):
        n = m * PIECES + j
        return remote(
            gin_ref.at[m, :, cut(j)], up.at[m, :, cut(j)], up_ss.at[n], up_rs.at[n],
            {"section": sec - 1},
        )

    def reduce_in(m, _):
        for y in range(rows):
            pre = dot_nn(x_ref[m, y], w1_ref[...]) + b1_ref[...]
            act, slope = silu_and_slope(pre)
            slope1[m, y] = slope
            act = act.astype(BF)
            act_pad[m, y + 1, pl.ds(PAD, cols)] = act.astype(F32)
            if y == 0:
                fe_out[m, 0] = act
            if y == rows - 1:
                fe_out[m, 1] = act
        return 0

    lax.fori_loop(0, micros, reduce_in, 0)

    greetings = (
        has_above.astype(jnp.int32) + has_below.astype(jnp.int32) + (sec > 0).astype(jnp.int32)
        + (sec < sections - 1).astype(jnp.int32) + (half - 1)
    )
    pl.semaphore_wait(barrier, greetings)

    @pl.when(has_above)
    def _():
        for m in range(micros):
            fe_up(m).start()

    @pl.when(has_below)
    def _():
        for m in range(micros):
            fe_down(m).start()

    def expand_out(m, _):
        @pl.when(has_above)
        def _():
            fe_down(m).wait_recv()
            act_pad[m, 0, pl.ds(PAD, cols)] = fe_in[m, 0].astype(F32)

        @pl.when(has_below)
        def _():
            fe_up(m).wait_recv()
            act_pad[m, rows + 1, pl.ds(PAD, cols)] = fe_in[m, 1].astype(F32)

        for shift in range(3):
            for y in range(rows + 2):
                taps[shift, m, y] = act_pad[m, y, pl.ds(PAD - 1 + shift, cols)].astype(BF)
        for y in range(rows):
            patch = jnp.concatenate(
                [taps[dx, m, y + dy] for dy in range(3) for dx in range(3)], axis=-1
            )
            pre = dot_nn(patch, w2_ref[...]) + b2_ref[...]
            act, slope = silu_and_slope(pre)
            slope2[m, y] = slope
            act = act.astype(BF)
            act2[m, y] = act
            for n in range(model // bottle):
                lanes = pl.ds(n * bottle, bottle)
                pre = dot_nn(act, w3_ref[:, lanes]) + b3_ref[:, lanes] + x_ref[m, y, :, lanes].astype(F32)
                slope3[m, y, :, lanes] = silu_and_slope(pre)[1]
        return 0

    lax.fori_loop(0, micros, expand_out, 0)

    def outer_part(m, j):
        @pl.when(jnp.logical_not(is_last))
        def _():
            relay(m, j).wait_recv()

        for y in range(rows):
            g3[y, cut(j)] = (up[m, y, cut(j)].astype(F32) * slope3[m, y, cut(j)]).astype(BF)
        back = dot_nt(g3[:, cut(j)].reshape(rows * width, model), w3_ref[...])
        g2 = (back.reshape(rows, width, bottle) * slope2[m, :, cut(j)]).astype(BF)
        g_pad[m, pl.ds(1, rows), pl.ds(PAD + j * width, width)] = g2.astype(F32)
        be_out[m, 0, cut(j)] = g2[0]
        be_out[m, 1, cut(j)] = g2[rows - 1]

        @pl.when(has_above)
        def _():
            be_up(m, j).start()

        @pl.when(has_below)
        def _():
            be_down(m, j).start()

    def take_rims(m, j):
        @pl.when(has_above)
        def _():
            be_down(m, j).wait_recv()
            g_pad[m, 0, pl.ds(PAD + j * width, width)] = be_in[m, 0, cut(j)].astype(F32)

        @pl.when(has_below)
        def _():
            be_up(m, j).wait_recv()
            g_pad[m, rows + 1, pl.ds(PAD + j * width, width)] = be_in[m, 1, cut(j)].astype(F32)

    def inner_part(m, j):
        total = jnp.zeros((rows * width, bottle), F32)
        for dx in range(3):
            moved = g_pad[m, :, pl.ds(PAD + 1 + j * width - dx, width)].astype(BF)
            for dy in range(3):
                piece = moved[2 - dy : 2 - dy + rows].reshape(rows * width, bottle)
                total = total + dot_nt(piece, w2_ref[pl.ds((3 * dy + dx) * bottle, bottle)])
        grad = (total.reshape(rows, width, bottle) * slope1[m, :, cut(j)]).astype(BF)
        g1[:, cut(j)] = grad
        for y in range(rows):
            direct = up[m, y, cut(j)].astype(F32) * slope3[m, y, cut(j)]
            gin_ref[m, y, cut(j)] = (dot_nt(grad[y], w1_ref[...]) + direct).astype(BF)

        @pl.when(sec > 0)
        def _():
            relay(m, j).start()

    def backward(m, _):
        @pl.when(is_last)
        def _():
            cot_copy(m).wait()

        outer_part(m, 0)
        take_rims(m, 0)
        for j in range(1, PIECES):
            outer_part(m, j)
            take_rims(m, j)
            inner_part(m, j - 1)
        inner_part(m, PIECES - 1)
        sum3[...] += dot_tn(act2[m].reshape(pixels, bottle), g3[...].reshape(pixels, model))
        g2 = g_pad[m, pl.ds(1, rows), pl.ds(PAD, cols)].astype(BF).reshape(pixels, bottle)
        for dy in range(3):
            for dx in range(3):
                patch = taps[dx, m, pl.ds(dy, rows)].reshape(pixels, bottle)
                sum2[pl.ds((3 * dy + dx) * bottle, bottle)] += dot_tn(patch, g2)
        sum1[...] += dot_tn(x_ref[m].reshape(pixels, model), g1[...].reshape(pixels, bottle))
        return 0

    lax.fori_loop(0, micros, backward, 0)

    kinds = (
        (sum3, p3, q3, r3, s3, o3_ref),
        (sum2, p2, q2, r2, s2, o2_ref),
        (sum1, p1, q1, r1, s1, o1_ref),
    )

    def swap(kind):
        total, sent, got, _, _, _ = kinds[kind]
        return remote(sent, got, a_ss.at[kind], a_rs.at[kind], {"tile": partner})

    def spread(kind, step):
        _, _, _, part, landed, _ = kinds[kind]
        there = lax.rem(zed + step, half)
        n = kind * half + step
        return remote(
            part.at[there], landed.at[step - 1], z_ss.at[n], z_rs.at[n], {"tile": there * 2 + core}
        )

    for kind, (total, sent, _, _, _, out) in enumerate(kinds):
        span = out.shape[0]
        for z in range(half):
            first = pl.multiple_of((2 * z + 1 - core) * span, 16)
            sent[z] = total[pl.ds(first, span)].astype(BF)
        swap(kind).start()
    for kind, (total, _, got, part, _, out) in enumerate(kinds):
        span = out.shape[0]
        swap(kind).wait_recv()
        for z in range(half):
            first = pl.multiple_of((2 * z + core) * span, 16)
            part[z] = (total[pl.ds(first, span)] + got[z].astype(F32)).astype(BF)
        for step in range(1, half):
            spread(kind, step).start()
        own = pl.multiple_of((2 * zed + core) * span, 16)
        out[...] = total[pl.ds(own, span)] + got[zed].astype(F32)
    for kind, (_, _, _, _, landed, out) in enumerate(kinds):
        value = out[...]
        for step in range(1, half):
            spread(kind, step).wait_recv()
            value = value + landed[step - 1].astype(F32)
        out[...] = value

    def close(m, _):
        @pl.when(has_above)
        def _():
            fe_up(m).wait_send()
            for j in range(PIECES):
                be_up(m, j).wait_send()

        @pl.when(has_below)
        def _():
            fe_down(m).wait_send()
            for j in range(PIECES):
                be_down(m, j).wait_send()

        @pl.when(sec > 0)
        def _():
            for j in range(PIECES):
                relay(m, j).wait_send()

        return 0

    lax.fori_loop(0, micros, close, 0)
    for kind in range(3):
        swap(kind).wait_send()
        for step in range(1, half):
            spread(kind, step).wait_send()


def local(
    sections, tiles,
    stored_inputs, cotangent, w_reduce, w_spatial, w_expand, bias_reduce, bias_spatial, bias_expand,
):
    _, micros, rows, cols, model = stored_inputs.shape
    bottle = w_reduce.shape[2]
    half = tiles // 2
    spans = (model // tiles, 9 * bottle // tiles, bottle // tiles)
    wides = (bottle, bottle, model)
    vmem = pltpu.VMEM
    dma = pltpu.SemaphoreType.DMA
    whole = pl.BlockSpec(memory_space=pltpu.VMEM)
    scratch = [
        vmem((micros, rows, cols, model), BF),
        vmem((micros, rows, cols, bottle), F32),
        vmem((micros, rows, cols, bottle), F32),
        vmem((micros, rows, cols, model), F32),
        vmem((micros, rows + 2, cols + 2 * PAD, bottle), F32),
        vmem((3, micros, rows + 2, cols, bottle), BF),
        vmem((micros, rows, cols, bottle), BF),
        vmem((micros, rows + 2, cols + 2 * PAD, bottle), F32),
        vmem((rows, cols, model), BF),
        vmem((rows, cols, bottle), BF),
    ]
    scratch += [vmem((micros, 2, cols, bottle), BF)] * 4
    scratch += [vmem((span * tiles, wide), F32) for span, wide in zip(spans, wides)]
    for count in (half, half, half, half - 1):
        scratch += [vmem((count, span, wide), BF) for span, wide in zip(spans, wides)]
    pieces = micros * PIECES
    scratch += [
        dma((micros,)), dma((pieces,)), dma((pieces,)), dma((micros, 2)), dma((micros, 2)),
        dma((pieces, 2)), dma((pieces, 2)), dma((3,)), dma((3,)), dma((3 * half,)), dma((3 * half,)),
    ]
    outs = pl.pallas_call(
        functools.partial(kernel, sections, tiles),
        out_shape=[jax.ShapeDtypeStruct((micros, rows, cols, model), BF)]
        + [jax.ShapeDtypeStruct((span, wide), F32) for span, wide in zip(spans, wides)],
        in_specs=[whole, pl.BlockSpec(memory_space=pl.ANY)] + [whole] * 6,
        out_specs=[whole] * 4,
        scratch_shapes=scratch,
        compiler_params=pltpu.CompilerParams(
            collective_id=0, has_side_effects=True, vmem_limit_bytes=66 * 1024 * 1000
        ),
    )(
        stored_inputs[0], cotangent, w_reduce[0], w_spatial[0], w_expand[0],
        bias_reduce, bias_spatial, bias_expand,
    )
    return tuple(out[None] for out in outs)


def solution(mesh):
    return jax.shard_map(
        functools.partial(local, mesh.shape["section"], mesh.shape["tile"]),
        mesh=mesh,
        in_specs=(
            P("section", None, "tile", None, None),
            P(None, "tile", None, None),
            P("section", None, None),
            P("section", None, None),
            P("section", None, None),
            P("section", None),
            P("section", None),
            P("section", None),
        ),
        out_specs=(
            P("section", None, "tile", None, None),
            P("section", "tile", None),
            P("section", "tile", None),
            P("section", "tile", None),
        ),
        check_vma=False,
    )
```

time: 431 us -> 175 us (0.41)
  waiting for transfers between devices: 205 us -> 0 us
  Pallas kernels: 0 us -> 168 us
  matrix products: 82.5 us -> 0 us
  other arithmetic: 53.7 us -> 0 us
  starting transfers between devices: 49.2 us -> 0 us
  local copies, waits for them, and re-layouts: 22.5 us -> 5.95 us
  between operations: 13.9 us -> 0.67 us
    pallas_call x0 -> x1, Pallas kernels: none -> 168 us  [local(): pl.pallas_call(functools.partial(kernel, sections, tiles), out_shape=[jax...]
    ppermute x23 -> x0, waiting for transfers between devices: 113 us -> none  [the longest x7 110 us: from_behind(): lax.ppermute(value, axis, [(source, source + steps) for source in range(l...]
    reduce_scatter x3 -> x0, waiting for transfers between devices: 91.9 us -> none  [the longest x1 32.2 us: local(): lax.psum_scatter(sum_two.astype(jnp.bfloat16), 'tile', scatter_dimension=...]
    dot_general x45 -> x0, matrix products: 82.5 us -> none  [the longest x21 46.9 us: contract_rows(): lax.dot_general(left_mat, right_mat, (((0,), (0,)), ((), ())), preferred_...]
    ppermute x23 -> x0, starting transfers between devices: 49.1 us -> none  [the longest x8 29.8 us: padded_2(): lax.ppermute(tail, axis, [(i, (i + 1) % count) for i in range(ends)])]
    select_n x14 -> x0, other arithmetic: 29 us -> none  [the longest x7 18.8 us: advance(): jnp.where(is_live, lax.dynamic_update_slice_in_dim(grads_in, input_grad[N...]
    mul x7 -> x0, other arithmetic: 14.3 us -> none  [advance(): upstream.reshape(pixels, model_w).astype(jnp.float32)]
    while x112 -> x0, local copies, waits for them, and re-layouts: 8.22 us -> none
  transfers between devices with their start and end apart: 26 -> 0, of which waited for: 11 -> 0; matrix products, arithmetic and copies ran while one was open for 17% -> 0% of each run, Pallas kernels for 0% -> 0%
where the time goes in v1:
time: 175 us; the launch traced here: 174 us
  Pallas kernels  168 us (96%)
  local copies, waits for them, and re-layouts  5.95 us (3%)
    pallas_call x1, Pallas kernels, local(): pl.pallas_call(functools.partial(kernel, sections, tiles), out_shape=[jax...  168 us
    unnamed x10, local copies, waits for them, and re-layouts  5.95 us

profile of v1, /device:TPU:0, one launch (start us, length us, event | category | flops | bytes accessed | tf_op | source)
XLA Modules:
  0.0 174.4 jit_solution(11102306371860005436)
XLA Ops:
  0.6 167.7 %shard_map.111 = (bf16[4,3,128,1024]{3,2,1,0:T(8,128)(2,1)}, f32[128,256]{1,0:T(8,128)}, f32[288,256]{1,0:T(8,128)}, f32[32,1024]{1,0:T(8,128)}) custom-call(bf16[4,3,128,1024]{3,2,1,0:T(8,128)(2,1)} %bitcast.8, bf16[4,3,128,1024]{3,2,1,0:T(8,128)(2,1)} %cot_ref.1, bf16[1024,256]{1,0:T(8,128)(2,1)} %bitcast.11, bf16[2304,256]{1,0:T(8,128)(2,1)} %bitcast.10, ...), custom_call_target="tpu_custom_call" | custom-call | tf_op jit(solution)/shard_map/pallas_call | solution.py:355
  168.4 0.0 copy-start.2
  168.4 0.0 copy-start
  168.4 0.0 copy-start.1
  168.4 3.9 %copy.16 = bf16[1,4,3,128,1024]{4,3,2,1,0:T(8,128)(2,1)} copy(bf16[1,4,3,128,1024]{4,3,2,1,0:T(8,128)(2,1)} %bitcast.9) | data formatting | bytes 6291456
  172.3 0.0 copy-done.2
  172.3 0.7 copy.17
  173.0 0.0 copy-done
  173.0 0.7 copy.18
  173.7 0.0 copy-done.1
  173.7 0.7 copy.19
Async XLA Ops:
  168.4 3.9 %copy-start.2 = (f32[128,256]{1,0:T(8,128)S(1)}, f32[128,256]{1,0:T(8,128)}, u32[]{:S(2)}) copy-start(f32[128,256]{1,0:T(8,128)} %get-tuple-element.9) | copy-start | bytes 393220
  168.4 4.6 %copy-start = (f32[288,256]{1,0:T(8,128)S(1)}, f32[288,256]{1,0:T(8,128)}, u32[]{:S(2)}) copy-start(f32[288,256]{1,0:T(8,128)} %get-tuple-element.10) | copy-start | bytes 884740
  168.4 5.3 %copy-start.1 = (f32[32,1024]{1,0:T(8,128)S(1)}, f32[32,1024]{1,0:T(8,128)}, u32[]{:S(2)}) copy-start(f32[32,1024]{1,0:T(8,128)} %get-tuple-element.11) | copy-start | bytes 393220

commit v2 on v1

--- a/solution.py
+++ b/solution.py
@@ -10,7 +10,8 @@
 BF = jnp.bfloat16
 F32 = jnp.float32
 PAD = 8
-PIECES = 4
+PIECES = 8
+LAG = 2
 
 
 def silu_and_slope(pre_act):
@@ -20,10 +21,6 @@
 
 def dot_nn(left, right):
     return jnp.dot(left, right, preferred_element_type=F32)
-
-
-def dot_nt(left, right):
-    return lax.dot_general(left, right, (((1,), (1,)), ((), ())), preferred_element_type=F32)
 
 
 def dot_tn(left, right):
@@ -34,7 +31,7 @@
     sections, tiles, x_ref, cot_ref, w1_ref, w2_ref, w3_ref, b1_ref, b2_ref, b3_ref,
     gin_ref, o1_ref, o2_ref, o3_ref,
     up, slope1, slope2, slope3, act_pad, taps, act2, g_pad, g3, g1,
-    fe_out, fe_in, be_out, be_in, sum1, sum2, sum3,
+    t1, t2, t3, fe_out, fe_in, be_out, be_in, sum1, sum2, sum3,
     p1, p2, p3, q1, q2, q3, r1, r2, r3, s1, s2, s3,
     cot_sem, up_ss, up_rs, fe_ss, fe_rs, be_ss, be_rs, a_ss, a_rs, z_ss, z_rs,
 ):
@@ -130,7 +127,7 @@
                 fe_out[m, 1] = act
         return 0
 
-    lax.fori_loop(0, micros, reduce_in, 0)
+    reduce_in(0, 0)
 
     greetings = (
         has_above.astype(jnp.int32) + has_below.astype(jnp.int32) + (sec > 0).astype(jnp.int32)
@@ -138,15 +135,29 @@
     )
     pl.semaphore_wait(barrier, greetings)
 
-    @pl.when(has_above)
-    def _():
-        for m in range(micros):
+    def share_rims(m):
+        @pl.when(has_above)
+        def _():
             fe_up(m).start()
 
-    @pl.when(has_below)
-    def _():
-        for m in range(micros):
+        @pl.when(has_below)
+        def _():
             fe_down(m).start()
+
+    def reduce_and_share(m, _):
+        reduce_in(m, 0)
+        share_rims(m)
+        return 0
+
+    share_rims(0)
+    for n in range(model // bottle):
+        lanes = pl.ds(n * bottle, bottle)
+        t1[:, lanes] = w1_ref[lanes, :].astype(F32).T.astype(BF)
+        t3[lanes, :] = w3_ref[:, lanes].astype(F32).T.astype(BF)
+    for n in range(9):
+        band = pl.ds(n * bottle, bottle)
+        t2[band, :] = w2_ref[band, :].astype(F32).T.astype(BF)
+    lax.fori_loop(1, micros, reduce_and_share, 0)
 
     def expand_out(m, _):
         @pl.when(has_above)
@@ -177,7 +188,9 @@
                 slope3[m, y, :, lanes] = silu_and_slope(pre)[1]
         return 0
 
-    lax.fori_loop(0, micros, expand_out, 0)
+    @pl.when(jnp.logical_not(is_last))
+    def _():
+        lax.fori_loop(0, micros, expand_out, 0)
 
     def outer_part(m, j):
         @pl.when(jnp.logical_not(is_last))
@@ -186,7 +199,7 @@
 
         for y in range(rows):
             g3[y, cut(j)] = (up[m, y, cut(j)].astype(F32) * slope3[m, y, cut(j)]).astype(BF)
-        back = dot_nt(g3[:, cut(j)].reshape(rows * width, model), w3_ref[...])
+        back = dot_nn(g3[:, cut(j)].reshape(rows * width, model), t3[...])
         g2 = (back.reshape(rows, width, bottle) * slope2[m, :, cut(j)]).astype(BF)
         g_pad[m, pl.ds(1, rows), pl.ds(PAD + j * width, width)] = g2.astype(F32)
         be_out[m, 0, cut(j)] = g2[0]
@@ -212,17 +225,26 @@
             g_pad[m, rows + 1, pl.ds(PAD + j * width, width)] = be_in[m, 1, cut(j)].astype(F32)
 
     def inner_part(m, j):
-        total = jnp.zeros((rows * width, bottle), F32)
-        for dx in range(3):
-            moved = g_pad[m, :, pl.ds(PAD + 1 + j * width - dx, width)].astype(BF)
-            for dy in range(3):
-                piece = moved[2 - dy : 2 - dy + rows].reshape(rows * width, bottle)
-                total = total + dot_nt(piece, w2_ref[pl.ds((3 * dy + dx) * bottle, bottle)])
+        moved = [
+            g_pad[m, :, pl.ds(PAD + 1 + j * width - dx, width)].astype(BF) for dx in range(3)
+        ]
+        patch = jnp.concatenate(
+            [
+                moved[dx][2 - dy : 2 - dy + rows].reshape(rows * width, bottle)
+                for dy in range(3)
+                for dx in range(3)
+            ],
+            axis=-1,
+        )
+        total = dot_nn(patch, t2[...])
         grad = (total.reshape(rows, width, bottle) * slope1[m, :, cut(j)]).astype(BF)
         g1[:, cut(j)] = grad
-        for y in range(rows):
-            direct = up[m, y, cut(j)].astype(F32) * slope3[m, y, cut(j)]
-            gin_ref[m, y, cut(j)] = (dot_nt(grad[y], w1_ref[...]) + direct).astype(BF)
+        flat = grad.reshape(rows * width, bottle)
+        for n in range(model // bottle):
+            lanes = pl.ds(n * bottle, bottle)
+            back = dot_nn(flat, t1[:, lanes]).reshape(rows, width, bottle)
+            direct = up[m, :, cut(j), lanes].astype(F32) * slope3[m, :, cut(j), lanes]
+            gin_ref[m, :, cut(j), lanes] = (back + direct).astype(BF)
 
         @pl.when(sec > 0)
         def _():
@@ -231,12 +253,16 @@
     def backward(m, _):
         @pl.when(is_last)
         def _():
+            expand_out(m, 0)
             cot_copy(m).wait()
 
-        outer_part(m, 0)
-        take_rims(m, 0)
-        for j in range(1, PIECES):
+        for j in range(PIECES):
             outer_part(m, j)
+            if j >= LAG:
+                take_rims(m, j - LAG)
+            if j > LAG:
+                inner_part(m, j - LAG - 1)
+        for j in range(PIECES - LAG, PIECES):
             take_rims(m, j)
             inner_part(m, j - 1)
         inner_part(m, PIECES - 1)
@@ -343,6 +369,7 @@
         vmem((rows, cols, model), BF),
         vmem((rows, cols, bottle), BF),
     ]
+    scratch += [vmem((bottle, model), BF), vmem((9 * bottle, bottle), BF), vmem((model, bottle), BF)]
     scratch += [vmem((micros, 2, cols, bottle), BF)] * 4
     scratch += [vmem((span * tiles, wide), F32) for span, wide in zip(spans, wides)]
     for count in (half, half, half, half - 1):

time: 175 us -> 150 us (0.86)
  Pallas kernels: 168 us -> 143 us
    pallas_call x1, Pallas kernels: 168 us -> 143 us  [local(): pl.pallas_call(functools.partial(kernel, sections, tiles), out_shape=[jax...]
where the time goes in v2:
time: 150 us; the launch traced here: 149 us
  Pallas kernels  143 us (95%)
  local copies, waits for them, and re-layouts  5.95 us (4%)
    pallas_call x1, Pallas kernels, local(): pl.pallas_call(functools.partial(kernel, sections, tiles), out_shape=[jax...  143 us
    unnamed x10, local copies, waits for them, and re-layouts  5.95 us

profile of v2, /device:TPU:0, one launch (start us, length us, event | category | flops | bytes accessed | tf_op | source)
XLA Modules:
  0.0 149.4 jit_solution(3086620537660416161)
XLA Ops:
  0.6 142.8 %shard_map.111 = (bf16[4,3,128,1024]{3,2,1,0:T(8,128)(2,1)}, f32[128,256]{1,0:T(8,128)}, f32[288,256]{1,0:T(8,128)}, f32[32,1024]{1,0:T(8,128)}) custom-call(bf16[4,3,128,1024]{3,2,1,0:T(8,128)(2,1)} %bitcast.8, bf16[4,3,128,1024]{3,2,1,0:T(8,128)(2,1)} %cot_ref.1, bf16[1024,256]{1,0:T(8,128)(2,1)} %bitcast.11, bf16[2304,256]{1,0:T(8,128)(2,1)} %bitcast.10, ...), custom_call_target="tpu_custom_call" | custom-call | tf_op jit(solution)/shard_map/pallas_call | solution.py:382
  143.5 0.0 copy-start.2
  143.5 0.0 copy-start
  143.5 0.0 copy-start.1
  143.5 3.9 %copy.16 = bf16[1,4,3,128,1024]{4,3,2,1,0:T(8,128)(2,1)} copy(bf16[1,4,3,128,1024]{4,3,2,1,0:T(8,128)(2,1)} %bitcast.9) | data formatting | bytes 6291456
  147.4 0.0 copy-done.2
  147.4 0.7 copy.17
  148.1 0.0 copy-done
  148.1 0.7 copy.18
  148.8 0.0 copy-done.1
  148.8 0.7 copy.19
Async XLA Ops:
  143.5 3.9 %copy-start.2 = (f32[128,256]{1,0:T(8,128)S(1)}, f32[128,256]{1,0:T(8,128)}, u32[]{:S(2)}) copy-start(f32[128,256]{1,0:T(8,128)} %get-tuple-element.9) | copy-start | bytes 393220
  143.5 4.6 %copy-start = (f32[288,256]{1,0:T(8,128)S(1)}, f32[288,256]{1,0:T(8,128)}, u32[]{:S(2)}) copy-start(f32[288,256]{1,0:T(8,128)} %get-tuple-element.10) | copy-start | bytes 884740
  143.5 5.3 %copy-start.1 = (f32[32,1024]{1,0:T(8,128)S(1)}, f32[32,1024]{1,0:T(8,128)}, u32[]{:S(2)}) copy-start(f32[32,1024]{1,0:T(8,128)} %get-tuple-element.11) | copy-start | bytes 393220

commit v3 on v2

--- a/solution.py
+++ b/solution.py
@@ -12,6 +12,8 @@
 PAD = 8
 PIECES = 8
 LAG = 2
+WIDE_OUTER = 4
+WIDE_INNER = 2
 
 
 def silu_and_slope(pre_act):
@@ -157,8 +159,6 @@
     for n in range(9):
         band = pl.ds(n * bottle, bottle)
         t2[band, :] = w2_ref[band, :].astype(F32).T.astype(BF)
-    lax.fori_loop(1, micros, reduce_and_share, 0)
-
     def expand_out(m, _):
         @pl.when(has_above)
         def _():
@@ -190,28 +190,32 @@
 
     @pl.when(jnp.logical_not(is_last))
     def _():
+        lax.fori_loop(1, micros, reduce_and_share, 0)
         lax.fori_loop(0, micros, expand_out, 0)
 
-    def outer_part(m, j):
-        @pl.when(jnp.logical_not(is_last))
-        def _():
+    def outer_part(m, j, count, awaited):
+        broad = count * width
+        here = pl.ds(j * width, broad)
+        if awaited:
             relay(m, j).wait_recv()
 
         for y in range(rows):
-            g3[y, cut(j)] = (up[m, y, cut(j)].astype(F32) * slope3[m, y, cut(j)]).astype(BF)
-        back = dot_nn(g3[:, cut(j)].reshape(rows * width, model), t3[...])
-        g2 = (back.reshape(rows, width, bottle) * slope2[m, :, cut(j)]).astype(BF)
-        g_pad[m, pl.ds(1, rows), pl.ds(PAD + j * width, width)] = g2.astype(F32)
-        be_out[m, 0, cut(j)] = g2[0]
-        be_out[m, 1, cut(j)] = g2[rows - 1]
+            g3[y, here] = (up[m, y, here].astype(F32) * slope3[m, y, here]).astype(BF)
+        back = dot_nn(g3[:, here].reshape(rows * broad, model), t3[...])
+        g2 = (back.reshape(rows, broad, bottle) * slope2[m, :, here]).astype(BF)
+        g_pad[m, pl.ds(1, rows), pl.ds(PAD + j * width, broad)] = g2.astype(F32)
+        be_out[m, 0, here] = g2[0]
+        be_out[m, 1, here] = g2[rows - 1]
 
         @pl.when(has_above)
         def _():
-            be_up(m, j).start()
+            for i in range(j, j + count):
+                be_up(m, i).start()
 
         @pl.when(has_below)
         def _():
-            be_down(m, j).start()
+            for i in range(j, j + count):
+                be_down(m, i).start()
 
     def take_rims(m, j):
         @pl.when(has_above)
@@ -224,54 +228,74 @@
             be_up(m, j).wait_recv()
             g_pad[m, rows + 1, pl.ds(PAD + j * width, width)] = be_in[m, 1, cut(j)].astype(F32)
 
-    def inner_part(m, j):
+    def inner_part(m, j, count):
+        broad = count * width
+        here = pl.ds(j * width, broad)
         moved = [
-            g_pad[m, :, pl.ds(PAD + 1 + j * width - dx, width)].astype(BF) for dx in range(3)
+            g_pad[m, :, pl.ds(PAD + 1 + j * width - dx, broad)].astype(BF) for dx in range(3)
         ]
         patch = jnp.concatenate(
             [
-                moved[dx][2 - dy : 2 - dy + rows].reshape(rows * width, bottle)
+                moved[dx][2 - dy : 2 - dy + rows].reshape(rows * broad, bottle)
                 for dy in range(3)
                 for dx in range(3)
             ],
             axis=-1,
         )
         total = dot_nn(patch, t2[...])
-        grad = (total.reshape(rows, width, bottle) * slope1[m, :, cut(j)]).astype(BF)
-        g1[:, cut(j)] = grad
-        flat = grad.reshape(rows * width, bottle)
+        grad = (total.reshape(rows, broad, bottle) * slope1[m, :, here]).astype(BF)
+        g1[:, here] = grad
+        flat = grad.reshape(rows * broad, bottle)
         for n in range(model // bottle):
             lanes = pl.ds(n * bottle, bottle)
-            back = dot_nn(flat, t1[:, lanes]).reshape(rows, width, bottle)
-            direct = up[m, :, cut(j), lanes].astype(F32) * slope3[m, :, cut(j), lanes]
-            gin_ref[m, :, cut(j), lanes] = (back + direct).astype(BF)
+            back = dot_nn(flat, t1[:, lanes]).reshape(rows, broad, bottle)
+            direct = up[m, :, here, lanes].astype(F32) * slope3[m, :, here, lanes]
+            gin_ref[m, :, here, lanes] = (back + direct).astype(BF)
 
         @pl.when(sec > 0)
         def _():
-            relay(m, j).start()
-
-    def backward(m, _):
-        @pl.when(is_last)
-        def _():
-            expand_out(m, 0)
-            cot_copy(m).wait()
-
-        for j in range(PIECES):
-            outer_part(m, j)
-            if j >= LAG:
-                take_rims(m, j - LAG)
-            if j > LAG:
-                inner_part(m, j - LAG - 1)
-        for j in range(PIECES - LAG, PIECES):
-            take_rims(m, j)
-            inner_part(m, j - 1)
-        inner_part(m, PIECES - 1)
+            for i in range(j, j + count):
+                relay(m, i).start()
+
+    def outer_sums(m):
         sum3[...] += dot_tn(act2[m].reshape(pixels, bottle), g3[...].reshape(pixels, model))
         g2 = g_pad[m, pl.ds(1, rows), pl.ds(PAD, cols)].astype(BF).reshape(pixels, bottle)
         for dy in range(3):
             for dx in range(3):
                 patch = taps[dx, m, pl.ds(dy, rows)].reshape(pixels, bottle)
                 sum2[pl.ds((3 * dy + dx) * bottle, bottle)] += dot_tn(patch, g2)
+
+    def backward(m, _):
+        @pl.when(is_last)
+        def _():
+            expand_out(m, 0)
+            cot_copy(m).wait()
+            for j in range(0, PIECES, WIDE_OUTER):
+                outer_part(m, j, WIDE_OUTER, False)
+
+            @pl.when(m < micros - 1)
+            def _():
+                reduce_and_share(m + 1, 0)
+
+            for j in range(PIECES):
+                take_rims(m, j)
+            for j in range(0, PIECES, WIDE_INNER):
+                inner_part(m, j, WIDE_INNER)
+
+        @pl.when(jnp.logical_not(is_last))
+        def _():
+            for j in range(PIECES):
+                outer_part(m, j, 1, True)
+                if j >= LAG:
+                    take_rims(m, j - LAG)
+                if j > LAG:
+                    inner_part(m, j - LAG - 1, 1)
+            for j in range(PIECES - LAG, PIECES):
+                take_rims(m, j)
+                inner_part(m, j - 1, 1)
+            inner_part(m, PIECES - 1, 1)
+
+        outer_sums(m)
         sum1[...] += dot_tn(x_ref[m].reshape(pixels, model), g1[...].reshape(pixels, bottle))
         return 0
 

time: 150 us -> 150 us (level)
  no operation moved by 1% of the time
where the time goes in v3:
time: 150 us
  Pallas kernels  143 us (95%)
  local copies, waits for them, and re-layouts  5.95 us (4%)
    pallas_call x1, Pallas kernels, local(): pl.pallas_call(functools.partial(kernel, sections, tiles), out_shape=[jax...  143 us
    unnamed x10, local copies, waits for them, and re-layouts  5.95 us

profile of v3, /device:TPU:0, one launch (start us, length us, event | category | flops | bytes accessed | tf_op | source)
XLA Modules:
  0.0 150.0 jit_solution(1687629173974951062)
XLA Ops:
  0.6 143.4 %shard_map.111 = (bf16[4,3,128,1024]{3,2,1,0:T(8,128)(2,1)}, f32[128,256]{1,0:T(8,128)}, f32[288,256]{1,0:T(8,128)}, f32[32,1024]{1,0:T(8,128)}) custom-call(bf16[4,3,128,1024]{3,2,1,0:T(8,128)(2,1)} %bitcast.8, bf16[4,3,128,1024]{3,2,1,0:T(8,128)(2,1)} %cot_ref.1, bf16[1024,256]{1,0:T(8,128)(2,1)} %bitcast.11, bf16[2304,256]{1,0:T(8,128)(2,1)} %bitcast.10, ...), custom_call_target="tpu_custom_call" | custom-call | tf_op jit(solution)/shard_map/pallas_call | solution.py:406
  144.0 0.0 copy-start.2
  144.0 0.0 copy-start
  144.0 0.0 copy-start.1
  144.0 3.9 %copy.16 = bf16[1,4,3,128,1024]{4,3,2,1,0:T(8,128)(2,1)} copy(bf16[1,4,3,128,1024]{4,3,2,1,0:T(8,128)(2,1)} %bitcast.9) | data formatting | bytes 6291456
  147.9 0.0 copy-done.2
  147.9 0.7 copy.17
  148.6 0.0 copy-done
  148.6 0.7 copy.18
  149.3 0.0 copy-done.1
  149.3 0.7 copy.19
Async XLA Ops:
  144.0 3.9 %copy-start.2 = (f32[128,256]{1,0:T(8,128)S(1)}, f32[128,256]{1,0:T(8,128)}, u32[]{:S(2)}) copy-start(f32[128,256]{1,0:T(8,128)} %get-tuple-element.9) | copy-start | bytes 393220
  144.0 4.6 %copy-start = (f32[288,256]{1,0:T(8,128)S(1)}, f32[288,256]{1,0:T(8,128)}, u32[]{:S(2)}) copy-start(f32[288,256]{1,0:T(8,128)} %get-tuple-element.10) | copy-start | bytes 884740
  144.0 5.3 %copy-start.1 = (f32[32,1024]{1,0:T(8,128)S(1)}, f32[32,1024]{1,0:T(8,128)}, u32[]{:S(2)}) copy-start(f32[32,1024]{1,0:T(8,128)} %get-tuple-element.11) | copy-start | bytes 393220
